TPU v7x, 256 devices: a whole 4x4x8 slice. The times are simulated.
256 devices in a mesh: line: 8 (over z_hi, core), dp: 32 (over z_lo, x, y).
Axes of the slice: x: 4, y: 4, z: 8 (z_hi: 4, z_lo: 2; z = z_hi * 2 + z_lo), core: 2. Of those that a mesh axis runs over, the one named last changes fastest.
Arguments:
- fields: bfloat16 [32, 4096, 128], P('dp', 'line'), may hold values from -6 to 6
- cotangent: bfloat16 [32, 4096, 128], P('dp', 'line'), may hold values from -6 to 6
- norm_gain: float32 [3, 128], replicated, may hold values from 0.1 to 1.9
- kernel: float32 [3, 15, 128], replicated, may hold values from -1.8 to 1.8
- mix_weight: bfloat16 [3, 128, 128], replicated, may hold values from -0.5 to 0.5
- line_order: int32 [3, 4096], P(None, 'line'), may hold values from 0 to 511, as said below
- line_starts: int32 [3, 32], P(None, 'line'), may hold values from 0 to 32
Outputs:
- imitated: bfloat16 [32, 4096, 128], P('dp', 'line')
- field_grad: bfloat16 [32, 4096, 128], P('dp', 'line')
- mix_grad: float32 [3, 128, 128], replicated
- kernel_grad: float32 [3, 15, 128], replicated
- gain_grad: float32 [3, 128], replicated
Inputs may be any that keep to these rules, and one draw needn't show every extreme that they name: For each direction, every aligned block of 512 entries of line_order is a permutation of 0 to 511.
All inputs are finite; a program needn't handle non-finite values.
Results may differ from a plain program's by a relative error of at most 0.014.
Values may be sent and summed in bfloat16 or wider, within the bound.
No kernel may reach another device: no remote copies, remote signals or barrier semaphores. Data moves between devices by JAX's collectives and lax.ppermute only.
A program may use at most 64 MiB of HBM per device.

v0:
```python
import jax
import jax.numpy as jnp
from jax import lax
from jax.sharding import PartitionSpec as P

LINE = 128
EPSILON = 1e-06


def tap_offsets():
    offsets = [0]
    for dilation_level in range(7):
        offsets = offsets + [-(2**dilation_level), 2**dilation_level]
    return offsets


def shifted(values, offset):
    if offset > 0:
        return jnp.concatenate([values[:, offset:], jnp.zeros_like(values[:, :offset])], axis=1)
    if offset < 0:
        return jnp.concatenate([jnp.zeros_like(values[:, offset:]), values[:, :offset]], axis=1)
    return values


def depthwise(inputs, weights):
    running = jnp.zeros(inputs.shape, jnp.float32)
    for tap_index, offset in enumerate(tap_offsets()):
        running = running + weights[tap_index] * shifted(inputs, offset)
    return running


def depthwise_transpose(grads, weights):
    running = jnp.zeros(grads.shape, jnp.float32)
    for tap_index, offset in enumerate(tap_offsets()):
        running = running + weights[tap_index] * shifted(grads, -offset)
    return running


def kernel_terms(grads, inputs):
    return jnp.stack(
        [jnp.sum(grads * shifted(inputs, offset), axis=(0, 1)) for offset in tap_offsets()]
    )


def block_view(array, line_count):
    batch_len, cell_count, channels = array.shape
    return array.reshape(batch_len, line_count, cell_count // line_count, channels)


def unpermute(array, table):
    return jnp.zeros_like(array).at[:, table].set(array)


def into_lines(array, table, shift, line_count):
    rolled = jnp.roll(block_view(array, line_count), shift, axis=1).reshape(array.shape)
    received = lax.all_to_all(rolled, "line", split_axis=1, concat_axis=1, tiled=True)
    return jnp.take(received, table, axis=1)


def out_of_lines(array, table, shift, line_count):
    placed = unpermute(array, table)
    received = lax.all_to_all(placed, "line", split_axis=1, concat_axis=1, tiled=True)
    return jnp.roll(block_view(received, line_count), -shift, axis=1).reshape(array.shape)


def norm_forward(stream, gain_row):
    values = stream.astype(jnp.float32)
    inverse = lax.rsqrt(jnp.mean(values * values, axis=-1, keepdims=True) + EPSILON)
    scaled = values * inverse
    normed = (scaled * gain_row).astype(jnp.bfloat16)
    return (values, inverse, scaled, normed)


def norm_backward(grad_cells, inverse, scaled, gain_row, grad_stream):
    cells_f = grad_cells.astype(jnp.float32)
    gain_part = jnp.sum(cells_f * scaled, axis=(0, 1))
    weighted = cells_f * gain_row
    grad_norm = inverse * (weighted - scaled * jnp.mean(weighted * scaled, axis=-1, keepdims=True))
    return (gain_part, (grad_stream.astype(jnp.float32) + grad_norm).astype(jnp.bfloat16))


def line_forward(regrouped, keep_mask, weights, mixing):
    channels = regrouped.shape[2]
    lined = regrouped.reshape(-1, LINE, channels)
    masked = jnp.where(keep_mask[:, :, None], lined, jnp.zeros_like(lined))
    hidden = depthwise(masked.astype(jnp.float32), weights)
    activated = jax.nn.silu(hidden).astype(jnp.bfloat16)
    mixed = jnp.dot(
        activated.reshape(-1, channels), mixing, preferred_element_type=jnp.float32
    ).astype(jnp.bfloat16)
    return (masked, hidden, activated, mixed.reshape(regrouped.shape))


def line_backward(grad_mixed, masked, hidden, activated, keep_mask, weights, mixing):
    channels = grad_mixed.shape[2]
    flat_grad = grad_mixed.reshape(-1, channels)
    mix_part = jnp.einsum(
        "nc,nd->cd", activated.reshape(-1, channels), flat_grad, preferred_element_type=jnp.float32
    )
    grad_act = jnp.einsum(
        "nd,cd->nc", flat_grad, mixing, preferred_element_type=jnp.float32
    ).reshape(hidden.shape)
    gate_value = jax.nn.sigmoid(hidden)
    grad_hidden = (grad_act * (gate_value * (1.0 + hidden * (1.0 - gate_value)))).astype(
        jnp.bfloat16
    )
    hidden_grad_f = grad_hidden.astype(jnp.float32)
    kernel_part = kernel_terms(hidden_grad_f, masked.astype(jnp.float32))
    grad_masked = depthwise_transpose(hidden_grad_f, weights)
    grad_normed = jnp.where(keep_mask[:, :, None], grad_masked, jnp.zeros_like(grad_masked)).astype(
        jnp.bfloat16
    )
    return (mix_part, kernel_part, grad_normed.reshape(grad_mixed.shape))


def body(fields, cotangent, norm_gain, kernel, mix_weight, line_order, line_starts):
    line_count = lax.axis_size("line")
    line_rank = lax.axis_index("line")
    batch_len = fields.shape[0]
    cell_count = fields.shape[1]
    positions = jnp.arange(LINE, dtype=jnp.int32)
    masks = [
        jnp.tile(positions[None, :] >= line_starts[direction][:, None], (batch_len, 1))
        for direction in range(3)
    ]
    grad_scale = float(lax.axis_size("dp") * batch_len * line_count * cell_count) ** (-0.5)
    collected = []

    def collect(mix_part, kernel_part, gain_part):
        collected.append((mix_part, kernel_part, gain_part))

    saved = []
    stream = fields
    for direction in range(3):
        values, inverse, scaled, normed = norm_forward(stream, norm_gain[direction])
        regrouped = into_lines(normed, line_order[direction], direction * line_rank, line_count)
        masked, hidden, activated, mixed = line_forward(
            regrouped, masks[direction], kernel[direction], mix_weight[direction]
        )
        returned = out_of_lines(mixed, line_order[direction], direction * line_rank, line_count)
        saved.append((inverse, scaled, masked, hidden, activated))
        stream = (values + returned.astype(jnp.float32)).astype(jnp.bfloat16)
    grad_stream = cotangent
    for direction in (2, 1, 0):
        inverse, scaled, masked, hidden, activated = saved[direction]
        grad_mixed = into_lines(
            grad_stream, line_order[direction], direction * line_rank, line_count
        )
        mix_part, kernel_part, grad_normed = line_backward(
            grad_mixed,
            masked,
            hidden,
            activated,
            masks[direction],
            kernel[direction],
            mix_weight[direction],
        )
        grad_cells = out_of_lines(
            grad_normed, line_order[direction], direction * line_rank, line_count
        )
        gain_part, grad_stream = norm_backward(
            grad_cells, inverse, scaled, norm_gain[direction], grad_stream
        )
        collect(mix_part, kernel_part, gain_part)
    ordered = collected[::-1]
    mix_stack = jnp.stack([entry[0] for entry in ordered])
    kernel_stack = jnp.stack([entry[1] for entry in ordered])
    gain_stack = jnp.stack([entry[2] for entry in ordered])
    mix_stack, kernel_stack, gain_stack = lax.psum(
        (mix_stack, kernel_stack, gain_stack), ("line", "dp")
    )
    return (
        stream,
        grad_stream,
        mix_stack * grad_scale,
        kernel_stack * grad_scale,
        gain_stack * grad_scale,
    )


def solution(mesh):
    in_specs = (
        P("dp", "line", None),
        P("dp", "line", None),
        P(),
        P(),
        P(),
        P(None, "line"),
        P(None, "line"),
    )
    out_specs = (P("dp", "line", None), P("dp", "line", None), P(), P(), P())
    return jax.shard_map(body, mesh=mesh, in_specs=in_specs, out_specs=out_specs, check_vma=False)
```

profile of v0, /device:TPU:1, one launch (start us, length us, event | category | flops | bytes accessed | tf_op | source)
XLA Modules:
  0.0 574.2 jit_solution(12604991823495048007)
XLA Ops:
  7.2 1.3 slice_bitcast_fusion.14
  8.5 1.1 fusion.69
  10.4 1.3 reduce.6
  12.4 10.1 %all-to-all-start = ((bf16[8,2,4096]{2,1,0:T(2,128)(2,1)}), bf16[8,2,4096]{2,1,0:T(2,128)(2,1)S(1)}, u32[]{:S(2)}, u32[]{:S(2)}) async-start(bf16[8,2,4096]{2,1,0:T(2,128)(2,1)} %reshape.868), calls=%async_computation | async-start | bytes 262144 | tf_op jit(solution)/shard_map/all_to_all | solution.py:56
  24.6 6.0 %all-to-all-done = bf16[8,2,4096]{2,1,0:T(2,128)(2,1)S(1)} async-done(((bf16[8,2,4096]{2,1,0:T(2,128)(2,1)}), bf16[8,2,4096]{2,1,0:T(2,128)(2,1)S(1)}, u32[]{:S(2)}, u32[]{:S(2)}) %all-to-all-start) | async-done | bytes 131104 | tf_op jit(solution)/shard_map/all_to_all | solution.py:56
  30.7 1.3 gather_fusion
  33.6 1.2 multiply_convert_fusion.2
  34.9 1.8 scatter_custom_fusion
  36.9 1.3 reduce.7
  38.9 4.8 all-to-all-start.1
  44.9 6.9 %all-to-all-done.1 = bf16[8,2,4096]{2,1,0:T(2,128)(2,1)S(1)} async-done(((bf16[8,2,4096]{2,1,0:T(2,128)(2,1)}), bf16[8,2,4096]{2,1,0:T(2,128)(2,1)S(1)}, u32[]{:S(2)}, u32[]{:S(2)}) %all-to-all-start.1) | async-done | bytes 131104 | tf_op jit(solution)/shard_map/all_to_all | solution.py:62
  52.5 1.3 reduce.8
  54.5 4.8 all-to-all-start.2
  60.0 7.4 %all-to-all-done.2 = bf16[8,2,4096]{2,1,0:T(2,128)(2,1)S(1)} async-done(((bf16[8,2,4096]{2,1,0:T(2,128)(2,1)}), bf16[8,2,4096]{2,1,0:T(2,128)(2,1)S(1)}, u32[]{:S(2)}, u32[]{:S(2)}) %all-to-all-start.2) | async-done | bytes 131104 | tf_op jit(solution)/shard_map/all_to_all | solution.py:56
  67.6 1.3 gather_fusion.1
  70.6 1.9 multiply_convert_fusion.1
  72.6 2.4 scatter_custom_fusion.1
  75.2 1.3 reduce.9
  77.2 4.9 all-to-all-start.3
  82.4 1.3 reduce.10
  84.4 5.8 %all-to-all-done.3 = bf16[8,2,4096]{2,1,0:T(2,128)(2,1)S(1)} async-done(((bf16[8,2,4096]{2,1,0:T(2,128)(2,1)}), bf16[8,2,4096]{2,1,0:T(2,128)(2,1)S(1)}, u32[]{:S(2)}, u32[]{:S(2)}) %all-to-all-start.3) | async-done | bytes 131104 | tf_op jit(solution)/shard_map/all_to_all | solution.py:62
  90.2 4.8 all-to-all-start.6
  96.5 1.3 reduce.11
  98.5 4.6 all-to-all-done.6
  103.1 5.4 all-to-all-start.4
  108.6 1.3 gather_fusion.3
  110.0 6.8 %all-to-all-done.4 = bf16[8,2,4096]{2,1,0:T(2,128)(2,1)} async-done(((bf16[8,2,4096]{2,1,0:T(2,128)(2,1)}), bf16[8,2,4096]{2,1,0:T(2,128)(2,1)}, u32[]{:S(2)}, u32[]{:S(2)}) %all-to-all-start.4) | async-done | bytes 131104 | tf_op jit(solution)/shard_map/all_to_all | solution.py:56
  116.8 1.4 reshape.877
  118.2 1.3 gather_fusion.2
  123.0 1.2 fusion.56
  130.7 2.7 scatter_custom_fusion.2
  133.3 1.8 copy.76
  135.1 2.9 reduce.13
  138.0 1.6 reshape.878
  139.6 5.3 all-to-all-start.5
  145.5 2.9 select_convert_fusion.2
  148.5 2.3 scatter_custom_fusion.3
  151.0 1.3 reduce.12
  153.2 7.0 %all-to-all-start.7 = ((bf16[8,2,4096]{2,1,0:T(2,128)(2,1)}), bf16[8,2,4096]{2,1,0:T(2,128)(2,1)S(1)}, u32[]{:S(2)}, u32[]{:S(2)}) async-start(bf16[8,2,4096]{2,1,0:T(2,128)(2,1)} %reshape.882), calls=%async_computation.7 | async-start | bytes 262144 | tf_op jit(solution)/shard_map/all_to_all | solution.py:62
  160.2 1.4 reshape.879
  162.3 6.0 %all-to-all-done.7 = bf16[8,2,4096]{2,1,0:T(2,128)(2,1)S(1)} async-done(((bf16[8,2,4096]{2,1,0:T(2,128)(2,1)}), bf16[8,2,4096]{2,1,0:T(2,128)(2,1)S(1)}, u32[]{:S(2)}, u32[]{:S(2)}) %all-to-all-start.7) | async-done | bytes 131104 | tf_op jit(solution)/shard_map/all_to_all | solution.py:62
  168.4 0.9 copy-done.27
  171.9 1.3 reduce.14
  173.3 12.0 %all_to_all.60 = bf16[8,2,4096]{2,1,0:T(2,128)(2,1)S(1)} all-to-all(bf16[8,2,4096]{2,1,0:T(2,128)(2,1)S(1)} %reshape.884), channel_id=1, replica_groups=mesh['line'=8,'dp'=32] {'line'}, dimensions={0} | all-to-all | bytes 262144 | tf_op jit(solution)/shard_map/all_to_all | solution.py:56
  186.1 1.9 gather_fusion.4
  188.0 1.1 bitcast_select_fusion.1
  189.8 2.9 fusion.54
  193.7 1.1 select_convert_fusion.1
  194.8 1.9 scatter_custom_fusion.4
  196.9 1.3 reduce.15
  199.0 4.8 all-to-all-start.9
  204.5 7.3 %all-to-all-done.9 = bf16[8,2,4096]{2,1,0:T(2,128)(2,1)S(1)} async-done(((bf16[8,2,4096]{2,1,0:T(2,128)(2,1)}), bf16[8,2,4096]{2,1,0:T(2,128)(2,1)S(1)}, u32[]{:S(2)}, u32[]{:S(2)}) %all-to-all-start.9) | async-done | bytes 131104 | tf_op jit(solution)/shard_map/all_to_all | solution.py:62
  213.8 1.3 reduce.16
  215.8 4.9 all-to-all-start.10
  223.5 5.3 all-to-all-done.10
  229.6 1.3 gather_fusion.5
  232.1 2.2 fusion.52
  237.4 1.9 select_convert_fusion
  239.3 2.1 scatter_custom_fusion.5
  241.7 1.3 reduce.17
  243.8 4.8 all-to-all-start.11
  249.3 236.4 %all-reduce.87.cloned.1.call-done = f32[3,128,128]{2,1,0:T(8,128)} async-done(((f32[3,128,128]{2,1,0:T(8,128)}), f32[3,128,128]{2,1,0:T(8,128)}) %all-reduce.87.cloned.1.call-update) | async-done | bytes 196624 | tf_op jit(solution)/shard_map/psum | solution.py:169
  485.8 1.6 broadcast_multiply_fusion
  489.0 76.0 %all-reduce.84 = (f32[3,15,128]{2,1,0:T(8,128)S(1)}, f32[3,128]{1,0:T(4,128)S(1)}) all-reduce(f32[3,15,128]{2,1,0:T(8,128)S(1)} %pad_maximum_fusion.1, f32[3,128]{1,0:T(4,128)S(1)} %pad_maximum_fusion.2), channel_id=1, replica_groups=mesh['line'=8,'dp'=32] {'line','dp'}, use_global_device_ids=true, to_apply=%region_58.62 | all-reduce | flops 6144 | bytes 49152 | tf_op jit(solution)/shard_map/psum | solution.py:169
  (475 shorter events, 48.9 us)
Async XLA Ops:
  8.5 43.6 %copy-start.48 = (f32[128]{0:T(128)}, f32[128]{0:T(128)S(1)}, u32[]{:S(2)}) copy-start(f32[128]{0:T(128)S(1)} %get-tuple-element.213) | copy-start | bytes 1540
  12.4 10.1 %copy-start.43 = (s32[3,512]{1,0:T(4,128)S(1)}, s32[3,512]{1,0:T(4,128)}, u32[]{:S(2)}) copy-start(s32[3,512]{1,0:T(4,128)} %param.18) | copy-start | bytes 18436
  12.4 10.1 %copy-start.42 = (f32[3,15,128]{2,1,0:T(8,128)S(1)}, f32[3,15,128]{2,1,0:T(8,128)}, u32[]{:S(2)}) copy-start(f32[3,15,128]{2,1,0:T(8,128)} %param.16) | copy-start | bytes 69124
  12.4 18.1 %all-to-all-start = ((bf16[8,2,4096]{2,1,0:T(2,128)(2,1)}), bf16[8,2,4096]{2,1,0:T(2,128)(2,1)S(1)}, u32[]{:S(2)}, u32[]{:S(2)}) async-start(bf16[8,2,4096]{2,1,0:T(2,128)(2,1)} %reshape.868), calls=%async_computation | async-start | bytes 262144 | tf_op jit(solution)/shard_map/all_to_all | solution.py:56
  22.5 9.5 %copy-start.82 = (pred[512]{0:T(512)(128)(4,1)}, pred[512]{0:T(512)(128)(4,1)S(1)}, u32[]{:S(2)}) copy-start(pred[512]{0:T(512)(128)(4,1)S(1)} %compare_and_fusion.2) | copy-start | bytes 1540
  23.1 9.6 %copy-start.59 = (f32[128]{0:T(128)}, f32[128]{0:T(128)S(1)}, u32[]{:S(2)}) copy-start(f32[128]{0:T(128)S(1)} %get-tuple-element.196) | copy-start | bytes 1540
  23.1 9.6 %copy-start.61 = (f32[128]{0:T(128)}, f32[128]{0:T(128)S(1)}, u32[]{:S(2)}) copy-start(f32[128]{0:T(128)S(1)} %get-tuple-element.197) | copy-start | bytes 1540
  23.1 9.6 %copy-start.63 = (f32[128]{0:T(128)}, f32[128]{0:T(128)S(1)}, u32[]{:S(2)}) copy-start(f32[128]{0:T(128)S(1)} %get-tuple-element.198) | copy-start | bytes 1540
  23.1 9.6 %copy-start.65 = (f32[128]{0:T(128)}, f32[128]{0:T(128)S(1)}, u32[]{:S(2)}) copy-start(f32[128]{0:T(128)S(1)} %get-tuple-element.199) | copy-start | bytes 1540
  23.1 9.7 %copy-start.67 = (f32[128]{0:T(128)}, f32[128]{0:T(128)S(1)}, u32[]{:S(2)}) copy-start(f32[128]{0:T(128)S(1)} %get-tuple-element.200) | copy-start | bytes 1540
  23.1 9.7 %copy-start.69 = (f32[128]{0:T(128)}, f32[128]{0:T(128)S(1)}, u32[]{:S(2)}) copy-start(f32[128]{0:T(128)S(1)} %get-tuple-element.201) | copy-start | bytes 1540
  23.8 9.0 %copy-start.73 = (f32[128]{0:T(128)}, f32[128]{0:T(128)S(1)}, u32[]{:S(2)}) copy-start(f32[128]{0:T(128)S(1)} %get-tuple-element.186) | copy-start | bytes 1540
  23.8 9.0 %copy-start.74 = (f32[128]{0:T(128)}, f32[128]{0:T(128)S(1)}, u32[]{:S(2)}) copy-start(f32[128]{0:T(128)S(1)} %get-tuple-element.187) | copy-start | bytes 1540
  23.8 9.0 %copy-start.75 = (f32[128]{0:T(128)}, f32[128]{0:T(128)S(1)}, u32[]{:S(2)}) copy-start(f32[128]{0:T(128)S(1)} %get-tuple-element.188) | copy-start | bytes 1540
  23.8 9.0 %copy-start.76 = (f32[128]{0:T(128)}, f32[128]{0:T(128)S(1)}, u32[]{:S(2)}) copy-start(f32[128]{0:T(128)S(1)} %get-tuple-element.189) | copy-start | bytes 1540
  23.8 9.0 %copy-start.77 = (f32[128]{0:T(128)}, f32[128]{0:T(128)S(1)}, u32[]{:S(2)}) copy-start(f32[128]{0:T(128)S(1)} %get-tuple-element.190) | copy-start | bytes 1540
  23.8 9.0 %copy-start.78 = (f32[128]{0:T(128)}, f32[128]{0:T(128)S(1)}, u32[]{:S(2)}) copy-start(f32[128]{0:T(128)S(1)} %get-tuple-element.191) | copy-start | bytes 1540
  23.8 9.0 %copy-start.79 = (f32[128]{0:T(128)}, f32[128]{0:T(128)S(1)}, u32[]{:S(2)}) copy-start(f32[128]{0:T(128)S(1)} %get-tuple-element.192) | copy-start | bytes 1540
  23.9 9.0 %copy-start.80 = (f32[128]{0:T(128)}, f32[128]{0:T(128)S(1)}, u32[]{:S(2)}) copy-start(f32[128]{0:T(128)S(1)} %get-tuple-element.193) | copy-start | bytes 1540
  23.9 9.0 %copy-start.81 = (f32[128]{0:T(128)}, f32[128]{0:T(128)S(1)}, u32[]{:S(2)}) copy-start(f32[128]{0:T(128)S(1)} %get-tuple-element.194) | copy-start | bytes 1540
  24.0 8.9 %copy-start.57 = (pred[4,128]{1,0:T(4,128)(4,1)}, pred[4,128]{1,0:T(4,128)(4,1)S(1)}, u32[]{:S(2)}) copy-start(pred[4,128]{1,0:T(4,128)(4,1)S(1)} %iota_compare_fusion.2) | copy-start | bytes 1540
  24.0 6.7 %copy-start.44 = (s32[1024]{0:T(1024)}, s32[1024]{0:T(1024)S(1)}, u32[]{:S(2)}) copy-start(s32[1024]{0:T(1024)S(1)} %pad_clamp_fusion.2) | copy-start | bytes 12292
  24.6 10.4 %copy-start.117 = (s32[512,1]{0,1:T(1,128)}, s32[512,1]{0,1:T(1,128)S(1)}, u32[]{:S(2)}) copy-start(s32[512,1]{0,1:T(1,128)S(1)} %get-tuple-element.206) | copy-start | bytes 6148
  38.9 12.9 %all-to-all-start.1 = ((bf16[8,2,4096]{2,1,0:T(2,128)(2,1)}), bf16[8,2,4096]{2,1,0:T(2,128)(2,1)S(1)}, u32[]{:S(2)}, u32[]{:S(2)}) async-start(bf16[8,2,4096]{2,1,0:T(2,128)(2,1)} %reshape.870), calls=%async_computation.1 | async-start | bytes 262144 | tf_op jit(solution)/shard_map/all_to_all | solution.py:62
  44.3 25.3 %copy-start.50 = (pred[4,128]{1,0:T(4,128)(4,1)}, pred[4,128]{1,0:T(4,128)(4,1)S(1)}, u32[]{:S(2)}) copy-start(pred[4,128]{1,0:T(4,128)(4,1)S(1)} %get-tuple-element.222) | copy-start | bytes 1540
  44.9 24.1 %copy-start.98 = (pred[512]{0:T(512)(128)(4,1)}, pred[512]{0:T(512)(128)(4,1)S(1)}, u32[]{:S(2)}) copy-start(pred[512]{0:T(512)(128)(4,1)S(1)} %get-tuple-element.220) | copy-start | bytes 1540
  54.5 12.9 %all-to-all-start.2 = ((bf16[8,2,4096]{2,1,0:T(2,128)(2,1)}), bf16[8,2,4096]{2,1,0:T(2,128)(2,1)S(1)}, u32[]{:S(2)}, u32[]{:S(2)}) async-start(bf16[8,2,4096]{2,1,0:T(2,128)(2,1)} %reshape.872), calls=%async_computation.2 | async-start | bytes 262144 | tf_op jit(solution)/shard_map/all_to_all | solution.py:56
  59.4 8.2 %copy-start.46 = (s32[1024]{0:T(1024)}, s32[1024]{0:T(1024)S(1)}, u32[]{:S(2)}) copy-start(s32[1024]{0:T(1024)S(1)} %pad_clamp_fusion.1) | copy-start | bytes 12292
  60.0 9.6 %copy-start.84 = (f32[128]{0:T(128)}, f32[128]{0:T(128)S(1)}, u32[]{:S(2)}) copy-start(f32[128]{0:T(128)S(1)} %get-tuple-element.170) | copy-start | bytes 1540
  60.0 9.6 %copy-start.86 = (f32[128]{0:T(128)}, f32[128]{0:T(128)S(1)}, u32[]{:S(2)}) copy-start(f32[128]{0:T(128)S(1)} %get-tuple-element.171) | copy-start | bytes 1540
  60.0 9.6 %copy-start.88 = (f32[128]{0:T(128)}, f32[128]{0:T(128)S(1)}, u32[]{:S(2)}) copy-start(f32[128]{0:T(128)S(1)} %get-tuple-element.172) | copy-start | bytes 1540
  60.0 9.6 %copy-start.90 = (f32[128]{0:T(128)}, f32[128]{0:T(128)S(1)}, u32[]{:S(2)}) copy-start(f32[128]{0:T(128)S(1)} %get-tuple-element.173) | copy-start | bytes 1540
  60.0 9.6 %copy-start.92 = (f32[128]{0:T(128)}, f32[128]{0:T(128)S(1)}, u32[]{:S(2)}) copy-start(f32[128]{0:T(128)S(1)} %get-tuple-element.174) | copy-start | bytes 1540
  60.0 9.6 %copy-start.94 = (f32[128]{0:T(128)}, f32[128]{0:T(128)S(1)}, u32[]{:S(2)}) copy-start(f32[128]{0:T(128)S(1)} %get-tuple-element.175) | copy-start | bytes 1540
  77.2 13.0 %all-to-all-start.3 = ((bf16[8,2,4096]{2,1,0:T(2,128)(2,1)}), bf16[8,2,4096]{2,1,0:T(2,128)(2,1)S(1)}, u32[]{:S(2)}, u32[]{:S(2)}) async-start(bf16[8,2,4096]{2,1,0:T(2,128)(2,1)} %reshape.874), calls=%async_computation.3 | async-start | bytes 262144 | tf_op jit(solution)/shard_map/all_to_all | solution.py:62
  90.2 12.9 %all-to-all-start.6 = ((bf16[8,2,4096]{2,1,0:T(2,128)(2,1)}), bf16[8,2,4096]{2,1,0:T(2,128)(2,1)S(1)}, u32[]{:S(2)}, u32[]{:S(2)}) async-start(bf16[8,2,4096]{2,1,0:T(2,128)(2,1)} %reshape.880), calls=%async_computation.6 | async-start | bytes 262144 | tf_op jit(solution)/shard_map/all_to_all | solution.py:56
  103.1 13.7 %all-to-all-start.4 = ((bf16[8,2,4096]{2,1,0:T(2,128)(2,1)}), bf16[8,2,4096]{2,1,0:T(2,128)(2,1)}, u32[]{:S(2)}, u32[]{:S(2)}) async-start(bf16[8,2,4096]{2,1,0:T(2,128)(2,1)} %reshape.876), calls=%async_computation.4 | async-start | bytes 262144 | tf_op jit(solution)/shard_map/all_to_all | solution.py:56
  139.6 13.6 %all-to-all-start.5 = ((bf16[8,2,4096]{2,1,0:T(2,128)(2,1)}), bf16[8,2,4096]{2,1,0:T(2,128)(2,1)}, u32[]{:S(2)}, u32[]{:S(2)}) async-start(bf16[8,2,4096]{2,1,0:T(2,128)(2,1)} %reshape.878), calls=%async_computation.5 | async-start | bytes 262144 | tf_op jit(solution)/shard_map/all_to_all | solution.py:62
  153.2 15.1 %all-to-all-start.7 = ((bf16[8,2,4096]{2,1,0:T(2,128)(2,1)}), bf16[8,2,4096]{2,1,0:T(2,128)(2,1)S(1)}, u32[]{:S(2)}, u32[]{:S(2)}) async-start(bf16[8,2,4096]{2,1,0:T(2,128)(2,1)} %reshape.882), calls=%async_computation.7 | async-start | bytes 262144 | tf_op jit(solution)/shard_map/all_to_all | solution.py:62
  198.2 5.6 copy-start.122
  198.2 5.6 copy-start.123
  198.2 5.6 copy-start.124
  198.2 5.6 copy-start.125
  198.2 5.6 copy-start.126
  198.3 5.6 copy-start.127
  198.3 5.6 copy-start.128
  198.3 5.6 copy-start.129
  198.3 5.6 copy-start.130
  198.3 5.6 copy-start.131
  198.3 5.6 copy-start.132
  198.3 5.6 copy-start.133
  199.0 12.9 %all-to-all-start.9 = ((bf16[8,2,4096]{2,1,0:T(2,128)(2,1)}), bf16[8,2,4096]{2,1,0:T(2,128)(2,1)S(1)}, u32[]{:S(2)}, u32[]{:S(2)}) async-start(bf16[8,2,4096]{2,1,0:T(2,128)(2,1)} %reshape.886), calls=%async_computation.9 | async-start | bytes 262144 | tf_op jit(solution)/shard_map/all_to_all | solution.py:62
  215.8 5.2 copy-start.26
  215.8 13.0 %all-to-all-start.10 = ((bf16[8,2,4096]{2,1,0:T(2,128)(2,1)}), bf16[8,2,4096]{2,1,0:T(2,128)(2,1)S(1)}, u32[]{:S(2)}, u32[]{:S(2)}) async-start(bf16[8,2,4096]{2,1,0:T(2,128)(2,1)} %reshape.888), calls=%async_computation.10 | async-start | bytes 262144 | tf_op jit(solution)/shard_map/all_to_all | solution.py:56
  220.7 265.0 %all-reduce.87.cloned.1.call-start = ((), (), s32[]{:S(2)}) async-start(), calls=%async_computation.12 | async-start | bytes 393216 | tf_op jit(solution)/shard_map/psum | solution.py:169
  243.7 5.0 copy-start.154
  243.7 5.0 copy-start.155
  243.7 5.0 copy-start.156
  243.7 5.0 copy-start.157
  243.7 5.0 copy-start.158
  243.7 5.0 copy-start.159
  243.8 5.0 copy-start.160
  243.8 5.0 copy-start.161
  243.8 243.6 %all-to-all-start.11 = ((bf16[8,2,4096]{2,1,0:T(2,128)(2,1)}), bf16[8,2,4096]{2,1,0:T(2,128)(2,1)S(1)}, u32[]{:S(2)}, u32[]{:S(2)}) async-start(bf16[8,2,4096]{2,1,0:T(2,128)(2,1)} %reshape.890), calls=%async_computation.11 | async-start | bytes 262144 | tf_op jit(solution)/shard_map/all_to_all | solution.py:62
  (110 other events, 128.9 us)
Sparse Core Ops, SparseCore 0:
  236.8 248.8 all-reduce.86
where the time goes:
time: 584 us; the launch traced here: 574 us
  waiting for transfers between devices  293 us (50%)
  blocking collectives  88 us (15%)
  local copies, waits for them, and re-layouts  65.5 us (11%)
  starting transfers between devices  61.9 us (11%)
  other arithmetic  39.9 us (7%)
  between operations  16.8 us (3%)
  matrix products  9.42 us (2%)
    psum x1, waiting for transfers between devices, body(): lax.psum((mix_stack, kernel_stack, gain_stack), ('line', 'dp'))  236 us
    psum x1, blocking collectives, body(): lax.psum((mix_stack, kernel_stack, gain_stack), ('line', 'dp'))  76 us
    all_to_all x6, starting transfers between devices, out_of_lines(): lax.all_to_all(placed, 'line', split_axis=1, concat_axis=1, tiled=True)  31.7 us
    all_to_all x5, starting transfers between devices, into_lines(): lax.all_to_all(rolled, 'line', split_axis=1, concat_axis=1, tiled=True)  30 us
    all_to_all x5, waiting for transfers between devices, into_lines(): lax.all_to_all(rolled, 'line', split_axis=1, concat_axis=1, tiled=True)  30 us
    unnamed x359, local copies, waits for them, and re-layouts  29.1 us
    all_to_all x6, waiting for transfers between devices, out_of_lines(): lax.all_to_all(placed, 'line', split_axis=1, concat_axis=1, tiled=True)  26.2 us
    unnamed x12, other arithmetic  17.3 us
  transfers between devices with their start and end apart: 12, of which 11 were waited for; matrix products, arithmetic and copies ran while one was open for 5% of the time, Pallas kernels for 0%

commit v1 on v0

--- a/solution.py
+++ b/solution.py
@@ -59,7 +59,10 @@
 
 def out_of_lines(array, table, shift, line_count):
     placed = unpermute(array, table)
-    received = lax.all_to_all(placed, "line", split_axis=1, concat_axis=1, tiled=True)
+    size = lax.axis_size("line")
+    tiles = jnp.stack(jnp.split(placed, size, axis=1), axis=0)
+    tiles = lax.all_to_all(tiles, "line", split_axis=0, concat_axis=0)
+    received = jnp.concatenate(tiles, axis=1)
     return jnp.roll(block_view(received, line_count), -shift, axis=1).reshape(array.shape)
 
 

time: 584 us -> 585 us (level); the launches traced: 574 us -> 583 us
  local copies, waits for them, and re-layouts: 65.5 us -> 84.3 us
  other arithmetic: 39.9 us -> 32.4 us
    unnamed x359 -> x381, local copies, waits for them, and re-layouts: 29.1 us -> 47.9 us
    unnamed x12 -> x6, other arithmetic: 17.3 us -> 8.22 us
    scatter x12 -> x6, local copies, waits for them, and re-layouts: 16 us -> 12.5 us  [unpermute(): return jnp.zeros_like(array).at[:, table].set(array)]
  transfers between devices with their start and end apart: 12 -> 12, of which waited for: 11 -> 10; matrix products, arithmetic and copies ran while one was open for 5% -> 6% of each run, Pallas kernels for 0% -> 0%
where the time goes in v1:
time: 585 us; the launch traced here: 583 us
  waiting for transfers between devices  291 us (50%)
  blocking collectives  88.2 us (15%)
  local copies, waits for them, and re-layouts  84.3 us (14%)
  starting transfers between devices  61.1 us (10%)
  other arithmetic  32.4 us (6%)
  between operations  16.4 us (3%)
  matrix products  9.42 us (2%)
    psum x1, waiting for transfers between devices, body(): lax.psum((mix_stack, kernel_stack, gain_stack), ('line', 'dp'))  234 us
    psum x1, blocking collectives, body(): lax.psum((mix_stack, kernel_stack, gain_stack), ('line', 'dp'))  76 us
    unnamed x381, local copies, waits for them, and re-layouts  47.9 us
    all_to_all x6, starting transfers between devices, out_of_lines(): tiles = lax.all_to_all(tiles, 'line', split_axis=0, concat_axis=0)  31.4 us
    all_to_all x5, waiting for transfers between devices, into_lines(): lax.all_to_all(rolled, 'line', split_axis=1, concat_axis=1, tiled=True)  30.4 us
    all_to_all x5, starting transfers between devices, into_lines(): lax.all_to_all(rolled, 'line', split_axis=1, concat_axis=1, tiled=True)  29.7 us
    all_to_all x6, waiting for transfers between devices, out_of_lines(): tiles = lax.all_to_all(tiles, 'line', split_axis=0, concat_axis=0)  27.4 us
    scatter x6, local copies, waits for them, and re-layouts, unpermute(): return jnp.zeros_like(array).at[:, table].set(array)  12.5 us
  transfers between devices with their start and end apart: 12, of which 10 were waited for; matrix products, arithmetic and copies ran while one was open for 6% of the time, Pallas kernels for 0%

profile of v1, /device:TPU:1, one launch (start us, length us, event | category | flops | bytes accessed | tf_op | source)
XLA Modules:
  0.0 583.1 jit_solution(1416312670809422318)
XLA Ops:
  8.0 1.1 fusion.69
  10.0 1.4 reduce.6
  12.0 10.1 %all-to-all-start = ((bf16[8,2,4096]{2,1,0:T(2,128)(2,1)}), bf16[8,2,4096]{2,1,0:T(2,128)(2,1)S(1)}, u32[]{:S(2)}, u32[]{:S(2)}) async-start(bf16[8,2,4096]{2,1,0:T(2,128)(2,1)} %reshape.868), calls=%async_computation | async-start | bytes 262144 | tf_op jit(solution)/shard_map/all_to_all | solution.py:56
  24.3 5.9 %all-to-all-done = bf16[8,2,4096]{2,1,0:T(2,128)(2,1)S(1)} async-done(((bf16[8,2,4096]{2,1,0:T(2,128)(2,1)}), bf16[8,2,4096]{2,1,0:T(2,128)(2,1)S(1)}, u32[]{:S(2)}, u32[]{:S(2)}) %all-to-all-start) | async-done | bytes 131104 | tf_op jit(solution)/shard_map/all_to_all | solution.py:56
  30.3 1.3 gather_fusion
  33.2 1.2 multiply_convert_fusion.2
  34.5 1.8 scatter_custom_fusion
  41.2 4.8 all-to-all-start.1
  47.1 7.0 %all-to-all-done.1 = bf16[8,1,64,128]{3,2,1,0:T(8,128)(2,1)S(1)} async-done(((bf16[8,1,64,128]{3,2,1,0:T(8,128)(2,1)}), bf16[8,1,64,128]{3,2,1,0:T(8,128)(2,1)S(1)}, u32[]{:S(2)}, u32[]{:S(2)}) %all-to-all-start.1) | async-done | bytes 131104 | tf_op jit(solution)/shard_map/all_to_all | solution.py:64
  54.7 1.4 reduce.7
  56.8 4.7 all-to-all-start.2
  62.8 6.9 %all-to-all-done.2 = bf16[8,2,4096]{2,1,0:T(2,128)(2,1)S(1)} async-done(((bf16[8,2,4096]{2,1,0:T(2,128)(2,1)}), bf16[8,2,4096]{2,1,0:T(2,128)(2,1)S(1)}, u32[]{:S(2)}, u32[]{:S(2)}) %all-to-all-start.2) | async-done | bytes 131104 | tf_op jit(solution)/shard_map/all_to_all | solution.py:56
  69.8 1.3 gather_fusion.1
  72.8 1.8 multiply_convert_fusion.1
  74.8 1.9 scatter_custom_fusion.1
  81.6 4.8 all-to-all-start.3
  86.7 1.4 reduce.8
  88.8 5.8 %all-to-all-done.3 = bf16[8,1,64,128]{3,2,1,0:T(8,128)(2,1)S(1)} async-done(((bf16[8,1,64,128]{3,2,1,0:T(8,128)(2,1)}), bf16[8,1,64,128]{3,2,1,0:T(8,128)(2,1)S(1)}, u32[]{:S(2)}, u32[]{:S(2)}) %all-to-all-start.3) | async-done | bytes 131104 | tf_op jit(solution)/shard_map/all_to_all | solution.py:64
  94.6 4.7 all-to-all-start.6
  100.0 1.4 reduce.9
  102.0 5.3 all-to-all-done.6
  107.3 5.4 all-to-all-start.4
  112.9 1.5 gather_fusion.3
  114.4 6.7 %all-to-all-done.4 = bf16[8,2,4096]{2,1,0:T(2,128)(2,1)} async-done(((bf16[8,2,4096]{2,1,0:T(2,128)(2,1)}), bf16[8,2,4096]{2,1,0:T(2,128)(2,1)}, u32[]{:S(2)}, u32[]{:S(2)}) %all-to-all-start.4) | async-done | bytes 131104 | tf_op jit(solution)/shard_map/all_to_all | solution.py:56
  121.0 1.4 reshape.873
  122.4 1.5 gather_fusion.2
  127.5 1.2 fusion.56
  131.0 0.8 fusion.141
  132.6 0.8 fusion.139
  134.3 0.8 convolution_convert_fusion
  135.1 2.7 scatter_custom_fusion.2
  137.8 1.4 constant_dynamic-update-slice_fusion.23
  139.2 1.3 constant_dynamic-update-slice_fusion.22
  140.5 1.3 constant_dynamic-update-slice_fusion.21
  141.8 1.3 constant_dynamic-update-slice_fusion.20
  145.6 5.3 all-to-all-start.5
  151.5 2.9 select_convert_fusion.2
  154.4 2.1 scatter_custom_fusion.3
  161.4 7.2 %all-to-all-start.7 = ((bf16[8,1,64,128]{3,2,1,0:T(8,128)(2,1)}), bf16[8,1,64,128]{3,2,1,0:T(8,128)(2,1)S(1)}, u32[]{:S(2)}, u32[]{:S(2)}) async-start(bf16[8,1,64,128]{3,2,1,0:T(8,128)(2,1)} %constant_dynamic-update-slice_fusion.24), calls=%async_computation.7 | async-start | bytes 262144 | tf_op jit(solution)/shard_map/all_to_all | solution.py:64
  168.6 0.9 fusion.85
  169.6 7.1 %all-to-all-done.7 = bf16[8,1,64,128]{3,2,1,0:T(8,128)(2,1)S(1)} async-done(((bf16[8,1,64,128]{3,2,1,0:T(8,128)(2,1)}), bf16[8,1,64,128]{3,2,1,0:T(8,128)(2,1)S(1)}, u32[]{:S(2)}, u32[]{:S(2)}) %all-to-all-start.7) | async-done | bytes 131104 | tf_op jit(solution)/shard_map/all_to_all | solution.py:64
  179.3 1.4 reduce.10
  180.7 12.2 %all_to_all.60 = bf16[8,2,4096]{2,1,0:T(2,128)(2,1)S(1)} all-to-all(bf16[8,2,4096]{2,1,0:T(2,128)(2,1)S(1)} %reshape.876), channel_id=1, replica_groups=mesh['line'=8,'dp'=32] {'line'}, dimensions={0} | all-to-all | bytes 262144 | tf_op jit(solution)/shard_map/all_to_all | solution.py:56
  193.1 1.9 gather_fusion.4
  195.0 1.1 bitcast_select_fusion.1
  196.7 2.9 fusion.54
  200.7 1.1 select_convert_fusion.1
  201.8 1.9 scatter_custom_fusion.4
  208.6 4.6 all-to-all-start.9
  213.9 7.4 %all-to-all-done.9 = bf16[8,1,64,128]{3,2,1,0:T(8,128)(2,1)S(1)} async-done(((bf16[8,1,64,128]{3,2,1,0:T(8,128)(2,1)}), bf16[8,1,64,128]{3,2,1,0:T(8,128)(2,1)S(1)}, u32[]{:S(2)}, u32[]{:S(2)}) %all-to-all-start.9) | async-done | bytes 131104 | tf_op jit(solution)/shard_map/all_to_all | solution.py:64
  223.2 1.4 reduce.11
  225.2 4.8 all-to-all-start.10
  230.2 0.8 convolution_bitcast_fusion
  231.7 0.8 convolution_bitcast_fusion.1
  232.6 5.6 all-to-all-done.10
  239.1 1.3 gather_fusion.5
  241.5 2.2 fusion.52
  246.9 1.9 select_convert_fusion
  248.8 2.1 scatter_custom_fusion.5
  255.9 4.7 all-to-all-start.11
  261.3 233.6 %all-reduce.87.cloned.1.call-done = f32[3,128,128]{2,1,0:T(8,128)} async-done(((f32[3,128,128]{2,1,0:T(8,128)}), f32[3,128,128]{2,1,0:T(8,128)}) %all-reduce.87.cloned.1.call-update) | async-done | bytes 196624 | tf_op jit(solution)/shard_map/psum | solution.py:172
  495.0 1.6 broadcast_multiply_fusion
  498.2 76.0 %all-reduce.84 = (f32[3,15,128]{2,1,0:T(8,128)S(1)}, f32[3,128]{1,0:T(4,128)S(1)}) all-reduce(f32[3,15,128]{2,1,0:T(8,128)S(1)} %pad_maximum_fusion.1, f32[3,128]{1,0:T(4,128)S(1)} %pad_maximum_fusion.2), channel_id=1, replica_groups=mesh['line'=8,'dp'=32] {'line','dp'}, use_global_device_ids=true, to_apply=%region_58.62 | all-reduce | flops 6144 | bytes 49152 | tf_op jit(solution)/shard_map/psum | solution.py:172
  575.4 0.9 fusion.65
  (490 shorter events, 64.7 us)
Async XLA Ops:
  8.0 46.3 %copy-start.48 = (f32[128]{0:T(128)}, f32[128]{0:T(128)S(1)}, u32[]{:S(2)}) copy-start(f32[128]{0:T(128)S(1)} %get-tuple-element.213) | copy-start | bytes 1540
  8.0 91.5 %copy-start.54 = (f32[128]{0:T(128)}, f32[128]{0:T(128)S(1)}, u32[]{:S(2)}) copy-start(f32[128]{0:T(128)S(1)} %get-tuple-element.211) | copy-start | bytes 1540
  12.0 10.1 %copy-start.43 = (s32[3,512]{1,0:T(4,128)S(1)}, s32[3,512]{1,0:T(4,128)}, u32[]{:S(2)}) copy-start(s32[3,512]{1,0:T(4,128)} %param.18) | copy-start | bytes 18436
  12.0 10.1 %copy-start.42 = (f32[3,15,128]{2,1,0:T(8,128)S(1)}, f32[3,15,128]{2,1,0:T(8,128)}, u32[]{:S(2)}) copy-start(f32[3,15,128]{2,1,0:T(8,128)} %param.16) | copy-start | bytes 69124
  12.0 18.1 %all-to-all-start = ((bf16[8,2,4096]{2,1,0:T(2,128)(2,1)}), bf16[8,2,4096]{2,1,0:T(2,128)(2,1)S(1)}, u32[]{:S(2)}, u32[]{:S(2)}) async-start(bf16[8,2,4096]{2,1,0:T(2,128)(2,1)} %reshape.868), calls=%async_computation | async-start | bytes 262144 | tf_op jit(solution)/shard_map/all_to_all | solution.py:56
  22.1 9.5 %copy-start.81 = (pred[512]{0:T(512)(128)(4,1)}, pred[512]{0:T(512)(128)(4,1)S(1)}, u32[]{:S(2)}) copy-start(pred[512]{0:T(512)(128)(4,1)S(1)} %compare_and_fusion.2) | copy-start | bytes 1540
  22.8 9.6 %copy-start.58 = (f32[128]{0:T(128)}, f32[128]{0:T(128)S(1)}, u32[]{:S(2)}) copy-start(f32[128]{0:T(128)S(1)} %get-tuple-element.196) | copy-start | bytes 1540
  22.8 9.6 %copy-start.60 = (f32[128]{0:T(128)}, f32[128]{0:T(128)S(1)}, u32[]{:S(2)}) copy-start(f32[128]{0:T(128)S(1)} %get-tuple-element.197) | copy-start | bytes 1540
  22.8 9.6 %copy-start.62 = (f32[128]{0:T(128)}, f32[128]{0:T(128)S(1)}, u32[]{:S(2)}) copy-start(f32[128]{0:T(128)S(1)} %get-tuple-element.198) | copy-start | bytes 1540
  22.8 9.6 %copy-start.64 = (f32[128]{0:T(128)}, f32[128]{0:T(128)S(1)}, u32[]{:S(2)}) copy-start(f32[128]{0:T(128)S(1)} %get-tuple-element.199) | copy-start | bytes 1540
  22.8 9.6 %copy-start.66 = (f32[128]{0:T(128)}, f32[128]{0:T(128)S(1)}, u32[]{:S(2)}) copy-start(f32[128]{0:T(128)S(1)} %get-tuple-element.200) | copy-start | bytes 1540
  22.8 9.6 %copy-start.68 = (f32[128]{0:T(128)}, f32[128]{0:T(128)S(1)}, u32[]{:S(2)}) copy-start(f32[128]{0:T(128)S(1)} %get-tuple-element.201) | copy-start | bytes 1540
  23.5 8.9 %copy-start.72 = (f32[128]{0:T(128)}, f32[128]{0:T(128)S(1)}, u32[]{:S(2)}) copy-start(f32[128]{0:T(128)S(1)} %get-tuple-element.186) | copy-start | bytes 1540
  23.5 8.9 %copy-start.73 = (f32[128]{0:T(128)}, f32[128]{0:T(128)S(1)}, u32[]{:S(2)}) copy-start(f32[128]{0:T(128)S(1)} %get-tuple-element.187) | copy-start | bytes 1540
  23.5 8.9 %copy-start.74 = (f32[128]{0:T(128)}, f32[128]{0:T(128)S(1)}, u32[]{:S(2)}) copy-start(f32[128]{0:T(128)S(1)} %get-tuple-element.188) | copy-start | bytes 1540
  23.5 8.9 %copy-start.75 = (f32[128]{0:T(128)}, f32[128]{0:T(128)S(1)}, u32[]{:S(2)}) copy-start(f32[128]{0:T(128)S(1)} %get-tuple-element.189) | copy-start | bytes 1540
  23.5 8.9 %copy-start.76 = (f32[128]{0:T(128)}, f32[128]{0:T(128)S(1)}, u32[]{:S(2)}) copy-start(f32[128]{0:T(128)S(1)} %get-tuple-element.190) | copy-start | bytes 1540
  23.5 8.9 %copy-start.77 = (f32[128]{0:T(128)}, f32[128]{0:T(128)S(1)}, u32[]{:S(2)}) copy-start(f32[128]{0:T(128)S(1)} %get-tuple-element.191) | copy-start | bytes 1540
  23.5 8.9 %copy-start.78 = (f32[128]{0:T(128)}, f32[128]{0:T(128)S(1)}, u32[]{:S(2)}) copy-start(f32[128]{0:T(128)S(1)} %get-tuple-element.192) | copy-start | bytes 1540
  23.5 8.9 %copy-start.79 = (f32[128]{0:T(128)}, f32[128]{0:T(128)S(1)}, u32[]{:S(2)}) copy-start(f32[128]{0:T(128)S(1)} %get-tuple-element.193) | copy-start | bytes 1540
  23.5 8.9 %copy-start.80 = (f32[128]{0:T(128)}, f32[128]{0:T(128)S(1)}, u32[]{:S(2)}) copy-start(f32[128]{0:T(128)S(1)} %get-tuple-element.194) | copy-start | bytes 1540
  23.6 8.8 %copy-start.56 = (pred[4,128]{1,0:T(4,128)(4,1)}, pred[4,128]{1,0:T(4,128)(4,1)S(1)}, u32[]{:S(2)}) copy-start(pred[4,128]{1,0:T(4,128)(4,1)S(1)} %iota_compare_fusion.2) | copy-start | bytes 1540
  23.6 6.7 %copy-start.44 = (s32[1024]{0:T(1024)}, s32[1024]{0:T(1024)S(1)}, u32[]{:S(2)}) copy-start(s32[1024]{0:T(1024)S(1)} %pad_clamp_fusion.2) | copy-start | bytes 12292
  24.3 10.2 %copy-start.115 = (s32[512,1]{0,1:T(1,128)}, s32[512,1]{0,1:T(1,128)S(1)}, u32[]{:S(2)}) copy-start(s32[512,1]{0,1:T(1,128)S(1)} %get-tuple-element.206) | copy-start | bytes 6148
  41.2 13.0 %all-to-all-start.1 = ((bf16[8,1,64,128]{3,2,1,0:T(8,128)(2,1)}), bf16[8,1,64,128]{3,2,1,0:T(8,128)(2,1)S(1)}, u32[]{:S(2)}, u32[]{:S(2)}) async-start(bf16[8,1,64,128]{3,2,1,0:T(8,128)(2,1)} %constant_dynamic-update-slice_fusion), calls=%async_computation.1 | async-start | bytes 262144 | tf_op jit(solution)/shard_map/all_to_all | solution.py:64
  46.6 25.3 %copy-start.50 = (pred[4,128]{1,0:T(4,128)(4,1)}, pred[4,128]{1,0:T(4,128)(4,1)S(1)}, u32[]{:S(2)}) copy-start(pred[4,128]{1,0:T(4,128)(4,1)S(1)} %get-tuple-element.224) | copy-start | bytes 1540
  47.1 24.1 %copy-start.97 = (pred[512]{0:T(512)(128)(4,1)}, pred[512]{0:T(512)(128)(4,1)S(1)}, u32[]{:S(2)}) copy-start(pred[512]{0:T(512)(128)(4,1)S(1)} %get-tuple-element.220) | copy-start | bytes 1540
  56.8 12.9 %all-to-all-start.2 = ((bf16[8,2,4096]{2,1,0:T(2,128)(2,1)}), bf16[8,2,4096]{2,1,0:T(2,128)(2,1)S(1)}, u32[]{:S(2)}, u32[]{:S(2)}) async-start(bf16[8,2,4096]{2,1,0:T(2,128)(2,1)} %reshape.870), calls=%async_computation.2 | async-start | bytes 262144 | tf_op jit(solution)/shard_map/all_to_all | solution.py:56
  62.7 9.2 %copy-start.83 = (f32[128]{0:T(128)}, f32[128]{0:T(128)S(1)}, u32[]{:S(2)}) copy-start(f32[128]{0:T(128)S(1)} %get-tuple-element.170) | copy-start | bytes 1540
  62.7 9.2 %copy-start.85 = (f32[128]{0:T(128)}, f32[128]{0:T(128)S(1)}, u32[]{:S(2)}) copy-start(f32[128]{0:T(128)S(1)} %get-tuple-element.171) | copy-start | bytes 1540
  62.7 9.2 %copy-start.87 = (f32[128]{0:T(128)}, f32[128]{0:T(128)S(1)}, u32[]{:S(2)}) copy-start(f32[128]{0:T(128)S(1)} %get-tuple-element.172) | copy-start | bytes 1540
  62.8 9.2 %copy-start.89 = (f32[128]{0:T(128)}, f32[128]{0:T(128)S(1)}, u32[]{:S(2)}) copy-start(f32[128]{0:T(128)S(1)} %get-tuple-element.173) | copy-start | bytes 1540
  62.8 9.2 %copy-start.91 = (f32[128]{0:T(128)}, f32[128]{0:T(128)S(1)}, u32[]{:S(2)}) copy-start(f32[128]{0:T(128)S(1)} %get-tuple-element.174) | copy-start | bytes 1540
  62.8 9.2 %copy-start.93 = (f32[128]{0:T(128)}, f32[128]{0:T(128)S(1)}, u32[]{:S(2)}) copy-start(f32[128]{0:T(128)S(1)} %get-tuple-element.175) | copy-start | bytes 1540
  81.6 13.0 %all-to-all-start.3 = ((bf16[8,1,64,128]{3,2,1,0:T(8,128)(2,1)}), bf16[8,1,64,128]{3,2,1,0:T(8,128)(2,1)S(1)}, u32[]{:S(2)}, u32[]{:S(2)}) async-start(bf16[8,1,64,128]{3,2,1,0:T(8,128)(2,1)} %constant_dynamic-update-slice_fusion.8), calls=%async_computation.3 | async-start | bytes 262144 | tf_op jit(solution)/shard_map/all_to_all | solution.py:64
  94.6 12.7 %all-to-all-start.6 = ((bf16[8,2,4096]{2,1,0:T(2,128)(2,1)}), bf16[8,2,4096]{2,1,0:T(2,128)(2,1)S(1)}, u32[]{:S(2)}, u32[]{:S(2)}) async-start(bf16[8,2,4096]{2,1,0:T(2,128)(2,1)} %reshape.874), calls=%async_computation.6 | async-start | bytes 262144 | tf_op jit(solution)/shard_map/all_to_all | solution.py:56
  107.3 13.7 %all-to-all-start.4 = ((bf16[8,2,4096]{2,1,0:T(2,128)(2,1)}), bf16[8,2,4096]{2,1,0:T(2,128)(2,1)}, u32[]{:S(2)}, u32[]{:S(2)}) async-start(bf16[8,2,4096]{2,1,0:T(2,128)(2,1)} %reshape.872), calls=%async_computation.4 | async-start | bytes 262144 | tf_op jit(solution)/shard_map/all_to_all | solution.py:56
  137.8 5.3 copy-start.27
  145.6 15.8 %all-to-all-start.5 = ((bf16[8,1,64,128]{3,2,1,0:T(8,128)(2,1)}), bf16[8,1,64,128]{3,2,1,0:T(8,128)(2,1)}, u32[]{:S(2)}, u32[]{:S(2)}) async-start(bf16[8,1,64,128]{3,2,1,0:T(8,128)(2,1)} %constant_dynamic-update-slice_fusion.16), calls=%async_computation.5 | async-start | bytes 262144 | tf_op jit(solution)/shard_map/all_to_all | solution.py:64
  161.4 15.3 %all-to-all-start.7 = ((bf16[8,1,64,128]{3,2,1,0:T(8,128)(2,1)}), bf16[8,1,64,128]{3,2,1,0:T(8,128)(2,1)S(1)}, u32[]{:S(2)}, u32[]{:S(2)}) async-start(bf16[8,1,64,128]{3,2,1,0:T(8,128)(2,1)} %constant_dynamic-update-slice_fusion.24), calls=%async_computation.7 | async-start | bytes 262144 | tf_op jit(solution)/shard_map/all_to_all | solution.py:64
  207.9 5.3 copy-start.120
  207.9 5.3 copy-start.121
  207.9 5.3 copy-start.122
  207.9 5.3 copy-start.123
  207.9 5.3 copy-start.124
  207.9 5.3 copy-start.125
  207.9 5.3 copy-start.126
  208.0 5.3 copy-start.127
  208.0 5.3 copy-start.128
  208.0 5.3 copy-start.129
  208.0 5.3 copy-start.130
  208.0 5.3 copy-start.131
  208.6 12.8 %all-to-all-start.9 = ((bf16[8,1,64,128]{3,2,1,0:T(8,128)(2,1)}), bf16[8,1,64,128]{3,2,1,0:T(8,128)(2,1)S(1)}, u32[]{:S(2)}, u32[]{:S(2)}) async-start(bf16[8,1,64,128]{3,2,1,0:T(8,128)(2,1)} %constant_dynamic-update-slice_fusion.32), calls=%async_computation.9 | async-start | bytes 262144 | tf_op jit(solution)/shard_map/all_to_all | solution.py:64
  225.2 13.0 %all-to-all-start.10 = ((bf16[8,2,4096]{2,1,0:T(2,128)(2,1)}), bf16[8,2,4096]{2,1,0:T(2,128)(2,1)S(1)}, u32[]{:S(2)}, u32[]{:S(2)}) async-start(bf16[8,2,4096]{2,1,0:T(2,128)(2,1)} %reshape.878), calls=%async_computation.10 | async-start | bytes 262144 | tf_op jit(solution)/shard_map/all_to_all | solution.py:56
  230.1 264.9 %all-reduce.87.cloned.1.call-start = ((), (), s32[]{:S(2)}) async-start(), calls=%async_computation.12 | async-start | bytes 393216 | tf_op jit(solution)/shard_map/psum | solution.py:172
  255.8 4.8 copy-start.152
  255.8 4.8 copy-start.153
  255.8 4.8 copy-start.154
  255.8 4.8 copy-start.155
  255.8 4.8 copy-start.156
  255.9 4.8 copy-start.157
  255.9 4.8 copy-start.158
  255.9 4.8 copy-start.159
  255.9 240.7 %all-to-all-start.11 = ((bf16[8,1,64,128]{3,2,1,0:T(8,128)(2,1)}), bf16[8,1,64,128]{3,2,1,0:T(8,128)(2,1)S(1)}, u32[]{:S(2)}, u32[]{:S(2)}) async-start(bf16[8,1,64,128]{3,2,1,0:T(8,128)(2,1)} %constant_dynamic-update-slice_fusion.40), calls=%async_computation.11 | async-start | bytes 262144 | tf_op jit(solution)/shard_map/all_to_all | solution.py:64
  (108 other events, 130.6 us)
Sparse Core Ops, SparseCore 0:
  246.3 248.6 all-reduce.86
